TPU v7x, 128 devices: a whole 4x4x4 slice. The times are simulated.
128 devices in a mesh: sx: 8 (over y, core), sy: 16 (over x, z).
Axes of the slice: x: 4, y: 4, z: 4, core: 2. Of those that a mesh axis runs over, the one named last changes fastest.
Arguments:
- loads: float32 [8, 16, 1536, 256], P('sx', 'sy')
- schur_flex: float32 [8, 16, 1536, 1536], P('sx', 'sy'), as said below
- dirichlet: float32 [8, 16, 1536, 1536], P('sx', 'sy'), as said below
- coupling: float32 [8, 16, 16, 1536], P('sx', 'sy'), may hold values from -0.3125 to 0.3125
- corner_index: int32 [8, 16, 16], P('sx', 'sy'), may hold values from 0 to 512, as said below
- face_lists: int32 [8, 16, 4, 384], P('sx', 'sy'), may hold values from 0 to 383, as said below
- coarse_inverse: float32 [512, 512], P(('sx', 'sy')), as said below
Outputs:
- multipliers: float32 [8, 16, 1536, 256], P('sx', 'sy')
- residual: float32 [8, 16, 1536, 256], P('sx', 'sy')
Inputs may be any that keep to these rules, and one draw needn't show every extreme that they name: `corner_index`: each subdomain lists 4 coarse dofs for each of its four corners; 512 marks a corner on the clamped edges of the panel, which has no coarse dof; every coarse dof below 512 is named by some subdomain. `face_lists`: each face's list is a permutation of the 384 dofs of the facing face; the facing lists of two neighbouring subdomains are inverse permutations. `schur_flex`: symmetric positive definite for every subdomain. `dirichlet`: symmetric positive definite for every subdomain. `coarse_inverse`: symmetric positive definite.
All inputs are finite; a program needn't handle non-finite values.
Results may differ from a plain program's by a relative error of at most 0.00017.
Values sent between devices are 32-bit elements; how exact they have to be, the bound alone decides.
A program may use at most 128 MiB of HBM per device.

v0:
```python
import jax
import jax.numpy as jnp
from jax import lax
from jax.sharding import PartitionSpec as P

HIGH = lax.Precision.HIGH
HIGHEST = lax.Precision.HIGHEST


def shifted(block, axis, distance):
    devices = range(lax.axis_size(axis))
    route = [(i - distance, i) for i in devices if i - distance in devices]
    return lax.ppermute(block, axis, route)


def facing(faces):
    return (
        shifted(faces[1], "sx", 1),
        shifted(faces[0], "sx", -1),
        shifted(faces[3], "sy", 1),
        shifted(faces[2], "sy", -1),
    )


def jump(field, match):
    size = field.shape[0] // 4
    faces = [field[f * size : (f + 1) * size] for f in range(4)]
    received = facing(faces)
    return jnp.concatenate(
        [faces[f] - jnp.dot(match[f], received[f], precision=HIGHEST) for f in range(4)], axis=0
    )


def inner(first, second):
    return jnp.sum(first * second, axis=0)


def shards(loads, schur_flex, dirichlet, coupling, corner_index, face_lists, coarse_inverse):
    flex_mat = schur_flex[0, 0]
    prec_mat = dirichlet[0, 0]
    coupling_mat = coupling[0, 0]
    corners = corner_index[0, 0]
    face_index = face_lists[0, 0]
    ncoarse = coarse_inverse.shape[1]
    ncl = corners.shape[0]
    size = face_index.shape[1]
    sx = lax.axis_index("sx")
    sy = lax.axis_index("sy")
    inside = jnp.stack([sx > 0, sx < lax.axis_size("sx") - 1, sy > 0, sy < lax.axis_size("sy") - 1])
    scale = jnp.repeat(1.0 + inside.astype(jnp.float32), size)[:, None]
    match = (face_index[:, :, None] == jnp.arange(size, dtype=jnp.int32)[None, None, :]).astype(
        jnp.float32
    )
    inverse = lax.all_gather(coarse_inverse, ("sx", "sy"), axis=0, tiled=True)
    slots = jnp.concatenate([corners, jnp.arange(ncoarse + 1, ncoarse + 4, dtype=jnp.int32)])
    place = (slots[None, :] == jnp.arange(ncoarse + 8, dtype=jnp.int32)[:, None]).astype(
        jnp.float32
    )
    coarse_ids = jnp.arange(ncoarse, dtype=jnp.float32)[None, :]
    own = corners.astype(jnp.float32)
    parts = [coupling_mat[:, f * size : (f + 1) * size].T for f in range(4)]
    tagged = [jnp.concatenate([part, jnp.broadcast_to(own, (8, ncl))], axis=0) for part in parts]
    pick = (own[:, None] == coarse_ids).astype(jnp.float32)
    columns = []
    for f, got in enumerate(facing(tagged)):
        their_pick = (got[size][:, None] == coarse_ids).astype(jnp.float32)
        theirs = jnp.dot(match[f], got[:size], precision=HIGHEST)
        columns.append(
            jnp.dot(parts[f], pick, precision=HIGHEST)
            - jnp.dot(theirs, their_pick, precision=HIGHEST)
        )
    coupling_jump = jnp.concatenate(columns, axis=0)

    def reduced(local_load, *rows):
        rows = list(rows) + [jnp.zeros_like(rows[0])] * (3 - len(rows))
        block = jnp.concatenate([local_load] + [row[None] for row in rows], axis=0)
        total = lax.psum(jnp.dot(place, block, precision=HIGHEST), ("sx", "sy"))
        return (total[:ncoarse], total[ncoarse + 1], total[ncoarse + 2], total[ncoarse + 3])

    def coarse(rhs):
        sol = jnp.dot(inverse, rhs, precision=HIGHEST)
        return (jnp.dot(coupling_jump, sol, precision=HIGHEST), inner(rhs, sol))

    def precondition(residual):
        spread = scale * residual
        applied = jnp.dot(prec_mat, spread, precision=HIGH)
        return (0.5 * jump(applied, match), 0.5 * inner(spread, applied))

    def flexible(direction):
        spread = scale * direction
        return (
            spread,
            jnp.dot(flex_mat, spread, precision=HIGH),
            jnp.dot(coupling_mat, spread, precision=HIGH),
        )

    residual = jump(loads[0, 0], match)
    direction, dot_part = precondition(residual)
    spread, flexed, load = flexible(direction)
    rhs, res_dot, energy, _ = reduced(load, dot_part, inner(spread, flexed))
    image = jump(flexed, match)
    correction, coarse_energy = coarse(rhs)
    step = res_dot / (energy + coarse_energy)
    residual = residual - step * (image + correction)
    multipliers = step * direction
    precond, dot_part = precondition(residual)
    spread, new_flexed, load = flexible(precond)
    new_rhs, new_dot, new_energy, cross = reduced(
        load, dot_part, inner(spread, new_flexed), inner(spread, flexed)
    )
    new_image = jump(new_flexed, match)
    beta = new_dot / res_dot
    rhs = new_rhs + beta * rhs
    energy = new_energy + beta * (2.0 * cross + beta * energy)
    correction, coarse_energy = coarse(rhs)
    step = new_dot / (energy + coarse_energy)
    multipliers = multipliers + step * (precond + beta * direction)
    residual = residual - step * (new_image + beta * image + correction)
    return (multipliers[None, None], residual[None, None])


def solution(mesh):
    return jax.shard_map(
        shards,
        mesh=mesh,
        in_specs=(
            P("sx", "sy", None, None),
            P("sx", "sy", None, None),
            P("sx", "sy", None, None),
            P("sx", "sy", None, None),
            P("sx", "sy", None),
            P("sx", "sy", None, None),
            P(("sx", "sy"), None),
        ),
        out_specs=(P("sx", "sy", None, None), P("sx", "sy", None, None)),
        check_vma=False,
    )
```

profile of v0, /device:TPU:1, one launch (start us, length us, event | category | flops | bytes accessed | tf_op | source)
XLA Modules:
  0.0 480.3 jit_solution(9736556489605518894)
XLA Ops:
  9.5 4.6 collective-permute-start.12
  14.1 1.9 collective-permute-start.13
  16.0 3.5 collective-permute-start.14
  21.0 2.5 slice_bitcast_fusion.6
  23.5 3.9 collective-permute-start
  31.2 1.9 collective-permute-start.1
  33.7 2.7 convolution_subtract_fusion
  36.4 4.3 collective-permute-start.2
  42.6 1.9 collective-permute-start.3
  49.7 5.8 %collective-permute-done.3 = f32[384,256]{1,0:T(8,128)S(1)} collective-permute-done((f32[384,256]{1,0:T(8,128)S(1)}, f32[384,256]{1,0:T(8,128)S(1)}, u32[]{:S(2)}, u32[]{:S(2)}) %collective-permute-start.3) | collective-permute-done | bytes 393248 | tf_op jit(solution)/shard_map/ppermute | solution.py:13
  56.1 4.1 multiply_reduce_fusion.4
  60.4 4.6 collective-permute-start.4
  66.4 3.4 collective-permute-start.6
  71.1 2.5 collective-permute-start.5
  74.2 4.1 collective-permute-done.6
  78.8 3.3 collective-permute-done.7
  83.3 4.2 multiply_reduce_fusion.3
  88.4 4.1 collective-permute-start.8
  92.5 5.6 %collective-permute-start.10 = (f32[384,256]{1,0:T(8,128)}, f32[384,256]{1,0:T(8,128)}, u32[]{:S(2)}, u32[]{:S(2)}) collective-permute-start(f32[384,256]{1,0:T(8,128)} %get-tuple-element.13), channel_id=1, source_target_pairs={{0,1},{1,2},{2,3},{3,4},{4,5},{5,6},{6,7},{7,8},{8,9},{9,10},{10,1... | collective-permute-start | bytes 1179656 | tf_op jit(solution)/shard_map/ppermute | solution.py:13
  99.4 1.9 collective-permute-start.9
  103.5 2.3 convolution_subtract_fusion.15
  106.0 2.3 convolution_subtract_fusion.13
  108.3 2.3 collective-permute-done.11
  110.7 2.3 convolution_subtract_fusion.12
  113.0 2.3 convolution_subtract_fusion.14
  115.3 1.6 reshape.275
  116.8 134.1 %all-reduce.3.cloned.1.call-done = f32[520,256]{1,0:T(8,128)} async-done(((f32[520,256]{1,0:T(8,128)}), f32[520,256]{1,0:T(8,128)}) %all-reduce.3.cloned.1.call-update) | async-done | bytes 532496 | tf_op jit(solution)/shard_map/psum | solution.py:77
  251.0 3.7 fusion.36
  254.7 2.0 copy.28
  258.8 5.7 %fusion.9 = f32[1536,256]{1,0:T(8,128)S(1)} fusion(f32[256,512]{1,0:T(8,128)} %fusion.36, f32[384,512]{1,0:T(8,128)} %convolution_subtract_fusion, f32[384,512]{1,0:T(8,128)} %convolution_subtract_fusion.1, f32[384,512]{1,0:T(8,128)} %convolution_subtract_fusion.2, f32[384,512]{1,0:T(8,128)} %convolution_subtract_fusion.3, ...), kind=kOutput, calls=%fused_computation.11 | convolution fusion | flops 2421817344 | bytes 8389632 | tf_op jit(solution)/shard_map/dot_general | solution.py:82
  264.6 7.4 %multiply_reduce_fusion.2 = (f32[256]{0:T(256)S(1)}, f32[1536,256]{1,0:T(8,128)S(1)}) fusion(f32[1536,256]{1,0:T(8,128)S(1)} %fusion.9, f32[1536]{0:T(1024)S(1)} %mul.194, f32[1,1,1536,1536]{3,2,1,0:T(8,128)} %param.9), kind=kOutput, calls=%fused_computation.34 | convolution fusion | flops 3625451264 | bytes 12590080 | tf_op jit(solution)/shard_map/dot_general | solution.py:86
  272.2 3.2 collective-permute-start.16
  275.3 1.9 collective-permute-start.18
  278.6 2.5 collective-permute-start.17
  281.6 4.1 collective-permute-done.18
  286.2 3.3 collective-permute-done.19
  290.7 5.8 %multiply_reduce_fusion.1 = (f32[256]{0:T(256)S(1)}, f32[256]{0:T(256)S(1)}, f32[1536,256]{1,0:T(8,128)}) fusion(f32[1536]{0:T(1024)S(1)} %broadcast_multiply_fusion, f32[384,256]{1,0:T(8,128)S(1)} %convolution_subtract_fusion.8, f32[384,256]{1,0:T(8,128)S(1)} %convolution_subtract_fusion.9, f32[384,256]{1,0:T(8,128)S(1)} %convolution_subtract_fusion.10, ...), kind=kOutput, calls=%fused_computation.33 | convolution fusion | flops 3628596736 | bytes 14163968 | tf_op jit(solution)/shard_map/dot_general | solution.py:93
  299.5 3.8 collective-permute-start.20
  303.3 3.9 collective-permute-start.22
  308.4 2.2 collective-permute-start.21
  310.6 139.0 %all-reduce.5.cloned.1.call-done = f32[520,256]{1,0:T(8,128)} async-done(((f32[520,256]{1,0:T(8,128)}), f32[520,256]{1,0:T(8,128)}) %all-reduce.5.cloned.1.call-update) | async-done | bytes 532496 | tf_op jit(solution)/shard_map/psum | solution.py:77
  450.4 3.9 fusion.40
  454.2 2.1 copy.31
  458.9 2.7 fusion.25
  461.6 1.7 convolution_subtract_fusion.7
  463.3 1.7 convolution_subtract_fusion.5
  465.0 1.7 convolution_subtract_fusion.4
  468.3 5.2 %fusion.29 = f32[1,1,1536,256]{3,2,1,0:T(8,128)} fusion(f32[1536,256]{1,0:T(8,128)S(1)} %copy-done.23, f32[384,256]{1,0:T(8,128)S(1)} %convolution_subtract_fusion.4, f32[384,256]{1,0:T(8,128)S(1)} %convolution_subtract_fusion.5, f32[384,256]{1,0:T(8,128)S(1)} %convolution_subtract_fusion.6, f32[384,256]{1,0:T(8,128)S(1)} %convolution_subtract_fusion.7, ...), kind=kOutput, calls=%fused_computation.31 | convolution fusion | flops 2422603776 | bytes 9963520 | tf_op jit(solution)/shard_map/dot_general | solution.py:82
  (173 shorter events, 39.8 us)
Async XLA Ops:
  7.2 108.1 %all-gather.3.cloned.1.call-start = ((), (), s32[]{:S(2)}) async-start(), calls=%async_computation.2 | async-start | bytes 1056768 | tf_op jit(solution)/shard_map/all_gather | solution.py:54
  7.9 243.1 %all-reduce.3.cloned.1.call-start = ((), (), s32[]{:S(2)}) async-start(), calls=%async_computation | async-start | bytes 1064960 | tf_op jit(solution)/shard_map/psum | solution.py:77
  9.5 36.9 %collective-permute-start.12 = (f32[392,16]{0,1:T(8,128)S(1)}, f32[392,16]{0,1:T(8,128)S(1)}, u32[]{:S(2)}, u32[]{:S(2)}) collective-permute-start(f32[392,16]{0,1:T(8,128)S(1)} %get-tuple-element.28), channel_id=1, source_target_pairs={{0,16},{16,32},{32,48},{48,64},{64,80},{80,96},{96,112},{1,17},{17... | collective-permute-start | bytes 75272 | tf_op jit(solution)/shard_map/ppermute | solution.py:13
  14.1 28.5 %collective-permute-start.13 = (f32[392,16]{0,1:T(8,128)S(1)}, f32[392,16]{0,1:T(8,128)S(1)}, u32[]{:S(2)}, u32[]{:S(2)}) collective-permute-start(f32[392,16]{0,1:T(8,128)S(1)} %get-tuple-element.29), channel_id=1, source_target_pairs={{16,0},{32,16},{48,32},{64,48},{80,64},{96,80},{112,96},{17,1},{33... | collective-permute-start | bytes 75272 | tf_op jit(solution)/shard_map/ppermute | solution.py:13
  16.0 20.4 %collective-permute-start.14 = (f32[392,16]{0,1:T(8,128)S(1)}, f32[392,16]{0,1:T(8,128)S(1)}, u32[]{:S(2)}, u32[]{:S(2)}) collective-permute-start(f32[392,16]{0,1:T(8,128)S(1)} %get-tuple-element.30), channel_id=1, source_target_pairs={{0,1},{1,2},{2,3},{3,4},{4,5},{5,6},{6,7},{7,8},{8,9},{9,10},{10,1... | collective-permute-start | bytes 75272 | tf_op jit(solution)/shard_map/ppermute | solution.py:13
  19.6 11.7 %collective-permute-start.15 = (f32[392,16]{0,1:T(8,128)S(1)}, f32[392,16]{0,1:T(8,128)S(1)}, u32[]{:S(2)}, u32[]{:S(2)}) collective-permute-start(f32[392,16]{0,1:T(8,128)S(1)} %get-tuple-element.31), channel_id=1, source_target_pairs={{1,0},{2,1},{3,2},{4,3},{5,4},{6,5},{7,6},{8,7},{9,8},{10,9},{11,1... | collective-permute-start | bytes 75272 | tf_op jit(solution)/shard_map/ppermute | solution.py:13
  23.5 23.4 %collective-permute-start = (f32[384,256]{1,0:T(8,128)}, f32[384,256]{1,0:T(8,128)}, u32[]{:S(2)}, u32[]{:S(2)}) collective-permute-start(f32[384,256]{1,0:T(8,128)} %get-tuple-element.20), channel_id=1, source_target_pairs={{0,16},{16,32},{32,48},{48,64},{64,80},{80,96},{96,112},{1,17},{17... | collective-permute-start | bytes 1179656 | tf_op jit(solution)/shard_map/ppermute | solution.py:13
  31.2 17.3 %collective-permute-start.1 = (f32[384,256]{1,0:T(8,128)}, f32[384,256]{1,0:T(8,128)S(1)}, u32[]{:S(2)}, u32[]{:S(2)}) collective-permute-start(f32[384,256]{1,0:T(8,128)} %get-tuple-element.21), channel_id=1, source_target_pairs={{16,0},{32,16},{48,32},{64,48},{80,64},{96,80},{112,96},{17,1},{33... | collective-permute-start | bytes 1179656 | tf_op jit(solution)/shard_map/ppermute | solution.py:13
  33.7 8.9 %copy-start.29 = (f32[384,256]{1,0:T(8,128)S(1)}, f32[384,256]{1,0:T(8,128)}, u32[]{:S(2)}) copy-start(f32[384,256]{1,0:T(8,128)} %get-tuple-element.23) | copy-start | bytes 1179652
  33.7 13.3 %copy-start.10 = (f32[1,1,1536,256]{3,2,1,0:T(8,128)S(1)}, f32[1,1,1536,256]{3,2,1,0:T(8,128)}, u32[]{:S(2)}) copy-start(f32[1,1,1536,256]{3,2,1,0:T(8,128)} %param.7) | copy-start | bytes 4718596
  36.4 12.7 %collective-permute-start.2 = (f32[384,256]{1,0:T(8,128)}, f32[384,256]{1,0:T(8,128)S(1)}, u32[]{:S(2)}, u32[]{:S(2)}) collective-permute-start(f32[384,256]{1,0:T(8,128)} %get-tuple-element.22), channel_id=1, source_target_pairs={{0,1},{1,2},{2,3},{3,4},{4,5},{5,6},{6,7},{7,8},{8,9},{9,10},{10,1... | collective-permute-start | bytes 1179656 | tf_op jit(solution)/shard_map/ppermute | solution.py:13
  40.8 15.3 %copy-start = (f32[1,1,1536,1536]{3,2,1,0:T(8,128)S(1)}, f32[1,1,1536,1536]{3,2,1,0:T(8,128)}, u32[]{:S(2)}) copy-start(f32[1,1,1536,1536]{3,2,1,0:T(8,128)} %param.9) | copy-start | bytes 28311556
  42.6 12.9 %collective-permute-start.3 = (f32[384,256]{1,0:T(8,128)S(1)}, f32[384,256]{1,0:T(8,128)S(1)}, u32[]{:S(2)}, u32[]{:S(2)}) collective-permute-start(f32[384,256]{1,0:T(8,128)S(1)} %copy-done.29), channel_id=1, source_target_pairs={{1,0},{2,1},{3,2},{4,3},{5,4},{6,5},{7,6},{8,7},{9,8},{10,9},{11,1... | collective-permute-start | bytes 1179656 | tf_op jit(solution)/shard_map/ppermute | solution.py:13
  49.1 11.1 %copy-start.18 = (f32[384,256]{1,0:T(8,128)}, f32[384,256]{1,0:T(8,128)S(1)}, u32[]{:S(2)}) copy-start(f32[384,256]{1,0:T(8,128)S(1)} %convolution_subtract_fusion.22) | copy-start | bytes 1179652
  49.7 10.6 %copy-start.19 = (f32[384,256]{1,0:T(8,128)}, f32[384,256]{1,0:T(8,128)S(1)}, u32[]{:S(2)}) copy-start(f32[384,256]{1,0:T(8,128)S(1)} %convolution_subtract_fusion.21) | copy-start | bytes 1179652
  56.1 27.2 %slice-start = ((s8[9437184]{0:T(1024)(128)(4,1)}), s8[4194304]{0:T(1024)(128)(4,1)S(1)}, s32[]{:S(2)}) async-start(s8[9437184]{0:T(1024)(128)(4,1)} %bitcast.172), calls=%async_computation.3 | async-start | bytes 8388608
  56.1 27.2 %slice-start.1 = ((s8[9437184]{0:T(1024)(128)(4,1)}), s8[1048576]{0:T(1024)(128)(4,1)S(1)}, s32[]{:S(2)}) async-start(s8[9437184]{0:T(1024)(128)(4,1)} %bitcast.172), calls=%async_computation.4 | async-start | bytes 2097152
  60.3 23.0 %slice-start.2 = ((s8[9437184]{0:T(1024)(128)(4,1)}), s8[4194304]{0:T(1024)(128)(4,1)S(1)}, s32[]{:S(2)}) async-start(s8[9437184]{0:T(1024)(128)(4,1)} %bitcast.172), calls=%async_computation.5 | async-start | bytes 8388608
  60.4 13.2 %collective-permute-start.4 = (f32[384,256]{1,0:T(8,128)S(1)}, f32[384,256]{1,0:T(8,128)S(1)}, u32[]{:S(2)}, u32[]{:S(2)}) collective-permute-start(f32[384,256]{1,0:T(8,128)S(1)} %get-tuple-element.16), channel_id=1, source_target_pairs={{0,16},{16,32},{32,48},{48,64},{64,80},{80,96},{96,112},{1,17},{17... | collective-permute-start | bytes 1179656 | tf_op jit(solution)/shard_map/ppermute | solution.py:13
  66.4 11.9 %collective-permute-start.6 = (f32[384,256]{1,0:T(8,128)S(1)}, f32[384,256]{1,0:T(8,128)S(1)}, u32[]{:S(2)}, u32[]{:S(2)}) collective-permute-start(f32[384,256]{1,0:T(8,128)S(1)} %get-tuple-element.17), channel_id=1, source_target_pairs={{0,1},{1,2},{2,3},{3,4},{4,5},{5,6},{6,7},{7,8},{8,9},{9,10},{10,1... | collective-permute-start | bytes 1179656 | tf_op jit(solution)/shard_map/ppermute | solution.py:13
  69.8 12.4 %collective-permute-start.7 = (f32[384,256]{1,0:T(8,128)S(1)}, f32[384,256]{1,0:T(8,128)S(1)}, u32[]{:S(2)}, u32[]{:S(2)}) collective-permute-start(f32[384,256]{1,0:T(8,128)S(1)} %get-tuple-element.18), channel_id=1, source_target_pairs={{1,0},{2,1},{3,2},{4,3},{5,4},{6,5},{7,6},{8,7},{9,8},{10,9},{11,1... | collective-permute-start | bytes 1179656 | tf_op jit(solution)/shard_map/ppermute | solution.py:13
  71.1 11.6 %collective-permute-start.5 = (f32[384,256]{1,0:T(8,128)S(1)}, f32[384,256]{1,0:T(8,128)S(1)}, u32[]{:S(2)}, u32[]{:S(2)}) collective-permute-start(f32[384,256]{1,0:T(8,128)S(1)} %get-tuple-element.19), channel_id=1, source_target_pairs={{16,0},{32,16},{48,32},{64,48},{80,64},{96,80},{112,96},{17,1},{33... | collective-permute-start | bytes 1179656 | tf_op jit(solution)/shard_map/ppermute | solution.py:13
  74.1 27.2 %copy-start.2 = (f32[384,256]{1,0:T(8,128)}, f32[384,256]{1,0:T(8,128)S(1)}, u32[]{:S(2)}) copy-start(f32[384,256]{1,0:T(8,128)S(1)} %convolution_subtract_fusion.19) | copy-start | bytes 1179652
  78.8 22.5 %copy-start.4 = (f32[384,256]{1,0:T(8,128)}, f32[384,256]{1,0:T(8,128)S(1)}, u32[]{:S(2)}) copy-start(f32[384,256]{1,0:T(8,128)S(1)} %convolution_subtract_fusion.17) | copy-start | bytes 1179652
  82.7 18.7 %copy-start.6 = (f32[384,256]{1,0:T(8,128)}, f32[384,256]{1,0:T(8,128)S(1)}, u32[]{:S(2)}) copy-start(f32[384,256]{1,0:T(8,128)S(1)} %convolution_subtract_fusion.16) | copy-start | bytes 1179652
  83.3 18.1 %copy-start.8 = (f32[384,256]{1,0:T(8,128)}, f32[384,256]{1,0:T(8,128)S(1)}, u32[]{:S(2)}) copy-start(f32[384,256]{1,0:T(8,128)S(1)} %convolution_subtract_fusion.18) | copy-start | bytes 1179652
  88.4 15.0 %collective-permute-start.8 = (f32[384,256]{1,0:T(8,128)}, f32[384,256]{1,0:T(8,128)}, u32[]{:S(2)}, u32[]{:S(2)}) collective-permute-start(f32[384,256]{1,0:T(8,128)} %get-tuple-element.12), channel_id=1, source_target_pairs={{0,16},{16,32},{32,48},{48,64},{64,80},{80,96},{96,112},{1,17},{17... | collective-permute-start | bytes 1179656 | tf_op jit(solution)/shard_map/ppermute | solution.py:13
  92.5 13.6 %collective-permute-start.10 = (f32[384,256]{1,0:T(8,128)}, f32[384,256]{1,0:T(8,128)}, u32[]{:S(2)}, u32[]{:S(2)}) collective-permute-start(f32[384,256]{1,0:T(8,128)} %get-tuple-element.13), channel_id=1, source_target_pairs={{0,1},{1,2},{2,3},{3,4},{4,5},{5,6},{6,7},{7,8},{8,9},{9,10},{10,1... | collective-permute-start | bytes 1179656 | tf_op jit(solution)/shard_map/ppermute | solution.py:13
  98.1 12.5 %collective-permute-start.11 = (f32[384,256]{1,0:T(8,128)S(1)}, f32[384,256]{1,0:T(8,128)}, u32[]{:S(2)}, u32[]{:S(2)}) collective-permute-start(f32[384,256]{1,0:T(8,128)S(1)} %get-tuple-element.14), channel_id=1, source_target_pairs={{1,0},{2,1},{3,2},{4,3},{5,4},{6,5},{7,6},{8,7},{9,8},{10,9},{11,1... | collective-permute-start | bytes 1179656 | tf_op jit(solution)/shard_map/ppermute | solution.py:13
  99.4 13.6 %collective-permute-start.9 = (f32[384,256]{1,0:T(8,128)S(1)}, f32[384,256]{1,0:T(8,128)}, u32[]{:S(2)}, u32[]{:S(2)}) collective-permute-start(f32[384,256]{1,0:T(8,128)S(1)} %get-tuple-element.15), channel_id=1, source_target_pairs={{16,0},{32,16},{48,32},{64,48},{80,64},{96,80},{112,96},{17,1},{33... | collective-permute-start | bytes 1179656 | tf_op jit(solution)/shard_map/ppermute | solution.py:13
  103.2 346.4 %all-reduce.5.cloned.1.call-start = ((), (), s32[]{:S(2)}) async-start(), calls=%async_computation.1 | async-start | bytes 1064960 | tf_op jit(solution)/shard_map/psum | solution.py:77
  264.5 26.1 %slice-start.3 = ((s8[9437184]{0:T(1024)(128)(4,1)}), s8[4194304]{0:T(1024)(128)(4,1)S(1)}, s32[]{:S(2)}) async-start(s8[9437184]{0:T(1024)(128)(4,1)} %bitcast.174), calls=%async_computation.6 | async-start | bytes 8388608
  264.6 26.1 %slice-start.4 = ((s8[9437184]{0:T(1024)(128)(4,1)}), s8[4194304]{0:T(1024)(128)(4,1)S(1)}, s32[]{:S(2)}) async-start(s8[9437184]{0:T(1024)(128)(4,1)} %bitcast.174), calls=%async_computation.7 | async-start | bytes 8388608
  272.0 18.6 %slice-start.5 = ((s8[9437184]{0:T(1024)(128)(4,1)}), s8[1048576]{0:T(1024)(128)(4,1)S(1)}, s32[]{:S(2)}) async-start(s8[9437184]{0:T(1024)(128)(4,1)} %bitcast.174), calls=%async_computation.8 | async-start | bytes 2097152
  272.2 8.9 %collective-permute-start.16 = (f32[384,256]{1,0:T(8,128)S(1)}, f32[384,256]{1,0:T(8,128)S(1)}, u32[]{:S(2)}, u32[]{:S(2)}) collective-permute-start(f32[384,256]{1,0:T(8,128)S(1)} %get-tuple-element.8), channel_id=1, source_target_pairs={{0,16},{16,32},{32,48},{48,64},{64,80},{80,96},{96,112},{1,17},{17... | collective-permute-start | bytes 1179656 | tf_op jit(solution)/shard_map/ppermute | solution.py:13
  275.3 10.4 %collective-permute-start.18 = (f32[384,256]{1,0:T(8,128)S(1)}, f32[384,256]{1,0:T(8,128)S(1)}, u32[]{:S(2)}, u32[]{:S(2)}) collective-permute-start(f32[384,256]{1,0:T(8,128)S(1)} %get-tuple-element.9), channel_id=1, source_target_pairs={{0,1},{1,2},{2,3},{3,4},{4,5},{5,6},{6,7},{7,8},{8,9},{9,10},{10,1... | collective-permute-start | bytes 1179656 | tf_op jit(solution)/shard_map/ppermute | solution.py:13
  277.3 12.2 %collective-permute-start.19 = (f32[384,256]{1,0:T(8,128)S(1)}, f32[384,256]{1,0:T(8,128)S(1)}, u32[]{:S(2)}, u32[]{:S(2)}) collective-permute-start(f32[384,256]{1,0:T(8,128)S(1)} %get-tuple-element.10), channel_id=1, source_target_pairs={{1,0},{2,1},{3,2},{4,3},{5,4},{6,5},{7,6},{8,7},{9,8},{10,9},{11,1... | collective-permute-start | bytes 1179656 | tf_op jit(solution)/shard_map/ppermute | solution.py:13
  278.6 11.5 %collective-permute-start.17 = (f32[384,256]{1,0:T(8,128)S(1)}, f32[384,256]{1,0:T(8,128)S(1)}, u32[]{:S(2)}, u32[]{:S(2)}) collective-permute-start(f32[384,256]{1,0:T(8,128)S(1)} %get-tuple-element.11), channel_id=1, source_target_pairs={{16,0},{32,16},{48,32},{64,48},{80,64},{96,80},{112,96},{17,1},{33... | collective-permute-start | bytes 1179656 | tf_op jit(solution)/shard_map/ppermute | solution.py:13
  281.6 14.8 %copy-start.11 = (f32[384,256]{1,0:T(8,128)}, f32[384,256]{1,0:T(8,128)S(1)}, u32[]{:S(2)}) copy-start(f32[384,256]{1,0:T(8,128)S(1)} %convolution_subtract_fusion.11) | copy-start | bytes 1179652
  286.2 10.2 %copy-start.13 = (f32[384,256]{1,0:T(8,128)}, f32[384,256]{1,0:T(8,128)S(1)}, u32[]{:S(2)}) copy-start(f32[384,256]{1,0:T(8,128)S(1)} %convolution_subtract_fusion.9) | copy-start | bytes 1179652
  299.5 162.1 %collective-permute-start.20 = (f32[384,256]{1,0:T(8,128)}, f32[384,256]{1,0:T(8,128)}, u32[]{:S(2)}, u32[]{:S(2)}) collective-permute-start(f32[384,256]{1,0:T(8,128)} %get-tuple-element.4), channel_id=1, source_target_pairs={{0,16},{16,32},{32,48},{48,64},{64,80},{80,96},{96,112},{1,17},{17... | collective-permute-start | bytes 1179656 | tf_op jit(solution)/shard_map/ppermute | solution.py:13
  303.3 160.0 %collective-permute-start.22 = (f32[384,256]{1,0:T(8,128)}, f32[384,256]{1,0:T(8,128)}, u32[]{:S(2)}, u32[]{:S(2)}) collective-permute-start(f32[384,256]{1,0:T(8,128)} %get-tuple-element.5), channel_id=1, source_target_pairs={{0,1},{1,2},{2,3},{3,4},{4,5},{5,6},{6,7},{7,8},{8,9},{9,10},{10,1... | collective-permute-start | bytes 1179656 | tf_op jit(solution)/shard_map/ppermute | solution.py:13
  307.2 157.8 %collective-permute-start.23 = (f32[384,256]{1,0:T(8,128)}, f32[384,256]{1,0:T(8,128)}, u32[]{:S(2)}, u32[]{:S(2)}) collective-permute-start(f32[384,256]{1,0:T(8,128)} %get-tuple-element.6), channel_id=1, source_target_pairs={{1,0},{2,1},{3,2},{4,3},{5,4},{6,5},{7,6},{8,7},{9,8},{10,9},{11,1... | collective-permute-start | bytes 1179656 | tf_op jit(solution)/shard_map/ppermute | solution.py:13
  308.4 158.2 %collective-permute-start.21 = (f32[384,256]{1,0:T(8,128)}, f32[384,256]{1,0:T(8,128)}, u32[]{:S(2)}, u32[]{:S(2)}) collective-permute-start(f32[384,256]{1,0:T(8,128)} %get-tuple-element.7), channel_id=1, source_target_pairs={{16,0},{32,16},{48,32},{64,48},{80,64},{96,80},{112,96},{17,1},{33... | collective-permute-start | bytes 1179656 | tf_op jit(solution)/shard_map/ppermute | solution.py:13
  458.8 9.4 %copy-start.30 = (f32[384,256]{1,0:T(8,128)S(1)}, f32[384,256]{1,0:T(8,128)}, u32[]{:S(2)}) copy-start(f32[384,256]{1,0:T(8,128)} %convolution_subtract_fusion.15) | copy-start | bytes 1179652
  458.8 9.4 %copy-start.31 = (f32[384,256]{1,0:T(8,128)S(1)}, f32[384,256]{1,0:T(8,128)}, u32[]{:S(2)}) copy-start(f32[384,256]{1,0:T(8,128)} %convolution_subtract_fusion.13) | copy-start | bytes 1179652
  458.9 9.4 %copy-start.32 = (f32[384,256]{1,0:T(8,128)S(1)}, f32[384,256]{1,0:T(8,128)}, u32[]{:S(2)}) copy-start(f32[384,256]{1,0:T(8,128)} %convolution_subtract_fusion.12) | copy-start | bytes 1179652
  458.9 9.4 %copy-start.33 = (f32[384,256]{1,0:T(8,128)S(1)}, f32[384,256]{1,0:T(8,128)}, u32[]{:S(2)}) copy-start(f32[384,256]{1,0:T(8,128)} %convolution_subtract_fusion.14) | copy-start | bytes 1179652
  (21 other events, 97.6 us)
Sparse Core Ops, SparseCore 0:
  10.8 72.5 all-gather.2
  103.3 147.5 all-reduce.2
  298.4 151.1 all-reduce.4
where the time goes:
time: 486 us; the launch traced here: 480 us
  waiting for transfers between devices  297 us (61%)
  matrix products  78.2 us (16%)
  starting transfers between devices  68.4 us (14%)
  between operations  15.1 us (3%)
  local copies, waits for them, and re-layouts  12.4 us (3%)
  other arithmetic  9.11 us (2%)
    psum x2, waiting for transfers between devices, reduced(): total = lax.psum(jnp.dot(place, block, precision=HIGHEST), ('sx', 'sy'))  273 us
    ppermute x24, starting transfers between devices, shifted(): return lax.ppermute(block, axis, route)  68.1 us
    ppermute x24, waiting for transfers between devices, shifted(): return lax.ppermute(block, axis, route)  23.2 us
    dot_general x20, matrix products, jump(): jnp.dot(match[f], received[f], precision=HIGHEST)  23.1 us
    dot_general x2, matrix products, precondition(): applied = jnp.dot(prec_mat, spread, precision=HIGH)  11.6 us
    dot_general x2, matrix products, coarse(): return (jnp.dot(coupling_jump, sol, precision=HIGHEST), inner(rhs, sol))  10.9 us
    dot_general x2, matrix products, flexible(): jnp.dot(flex_mat, spread, precision=HIGH)  9.93 us
  transfers between devices with their start and end apart: 27, of which 9 were waited for; matrix products, arithmetic and copies ran while one was open for 13% of the time, Pallas kernels for 0%

commit v1 on v0

--- a/solution.py
+++ b/solution.py
@@ -74,7 +74,9 @@
     def reduced(local_load, *rows):
         rows = list(rows) + [jnp.zeros_like(rows[0])] * (3 - len(rows))
         block = jnp.concatenate([local_load] + [row[None] for row in rows], axis=0)
-        total = lax.psum(jnp.dot(place, block, precision=HIGHEST), ("sx", "sy"))
+        total = jnp.sum(
+            lax.all_gather(jnp.dot(place, block, precision=HIGHEST), ("sx", "sy")), axis=0
+        )
         return (total[:ncoarse], total[ncoarse + 1], total[ncoarse + 2], total[ncoarse + 3])
 
     def coarse(rhs):

time: 486 us -> 558 us (1.15)
  other arithmetic: 9.11 us -> 47.4 us
  waiting for transfers between devices: 297 us -> 334 us
    all_gather x0 -> x2, waiting for transfers between devices: none -> 294 us  [reduced(): lax.all_gather(jnp.dot(place, block, precision=HIGHEST), ('sx', 'sy'))]
    psum x2 -> x0, waiting for transfers between devices: 273 us -> none  [reduced(): total = lax.psum(jnp.dot(place, block, precision=HIGHEST), ('sx', 'sy'))]
    reduce_sum x2, other arithmetic: 2.87 us -> 43.1 us  [reduced(): jnp.sum(lax.all_gather(jnp.dot(place, block, precision=HIGHEST), ('sx', '...]
    ppermute x24, waiting for transfers between devices: 23.2 us -> 39.5 us  [shifted(): return lax.ppermute(block, axis, route)]
  transfers between devices with their start and end apart: 27 -> 27, of which waited for: 9 -> 13; matrix products, arithmetic and copies ran while one was open for 13% -> 9% of each run, Pallas kernels for 0% -> 0%
where the time goes in v1:
time: 558 us; the launch traced here: 551 us
  waiting for transfers between devices  334 us (60%)
  matrix products  75.6 us (14%)
  starting transfers between devices  69.9 us (13%)
  other arithmetic  47.4 us (8%)
  between operations  15.1 us (3%)
  local copies, waits for them, and re-layouts  9.32 us (2%)
    all_gather x2, waiting for transfers between devices, reduced(): lax.all_gather(jnp.dot(place, block, precision=HIGHEST), ('sx', 'sy'))  294 us
    ppermute x24, starting transfers between devices, shifted(): return lax.ppermute(block, axis, route)  69.8 us
    reduce_sum x2, other arithmetic, reduced(): jnp.sum(lax.all_gather(jnp.dot(place, block, precision=HIGHEST), ('sx', '...  43.1 us
    ppermute x24, waiting for transfers between devices, shifted(): return lax.ppermute(block, axis, route)  39.5 us
    dot_general x20, matrix products, jump(): jnp.dot(match[f], received[f], precision=HIGHEST)  21.1 us
    dot_general x2, matrix products, precondition(): applied = jnp.dot(prec_mat, spread, precision=HIGH)  15.4 us
    dot_general x2, matrix products, coarse(): return (jnp.dot(coupling_jump, sol, precision=HIGHEST), inner(rhs, sol))  11.6 us
  transfers between devices with their start and end apart: 27, of which 13 were waited for; matrix products, arithmetic and copies ran while one was open for 9% of the time, Pallas kernels for 0%

profile of v1, /device:TPU:1, one launch (start us, length us, event | category | flops | bytes accessed | tf_op | source)
XLA Modules:
  0.0 551.1 jit_solution(760302953178114721)
XLA Ops:
  7.2 2.3 slice_bitcast_fusion.6
  10.8 5.8 %collective-permute-start.2 = (f32[384,256]{1,0:T(8,128)S(1)}, f32[384,256]{1,0:T(8,128)}, u32[]{:S(2)}, u32[]{:S(2)}) collective-permute-start(f32[384,256]{1,0:T(8,128)S(1)} %get-tuple-element.22), channel_id=1, source_target_pairs={{0,1},{1,2},{2,3},{3,4},{4,5},{5,6},{6,7},{7,8},{8,9},{9,10},{10,1... | collective-permute-start | bytes 1179656 | tf_op jit(solution)/shard_map/ppermute | solution.py:13
  16.6 2.9 collective-permute-start.1
  19.5 3.2 collective-permute-start
  23.5 1.5 convolution_subtract_fusion.20
  25.1 1.6 convolution_subtract_fusion.21
  26.8 1.6 convolution_subtract_fusion.22
  28.4 1.6 convolution_subtract_fusion.23
  30.1 8.0 %multiply_reduce_fusion.4 = (f32[256]{0:T(256)S(1)}, f32[1536,256]{1,0:T(8,128)S(1)}) fusion(f32[1536]{0:T(1024)S(1)} %mul.194, f32[384,256]{1,0:T(8,128)S(1)} %convolution_subtract_fusion.20, f32[384,256]{1,0:T(8,128)S(1)} %convolution_subtract_fusion.21, f32[384,256]{1,0:T(8,128)S(1)} %convolution_subtract_fusion.22, ...), kind=kOutput, calls=%fused_computation.36 | convolution fusion | flops 3627810560 | bytes 12590080 | tf_op jit(solution)/shard_map/dot_general | solution.py:88
  38.3 4.0 collective-permute-start.4
  42.3 1.9 collective-permute-start.5
  44.2 3.6 collective-permute-start.6
  47.8 1.8 collective-permute-start.7
  50.2 1.5 collective-permute-done.5
  52.2 2.5 collective-permute-done.6
  55.3 4.1 collective-permute-done.7
  60.6 4.2 multiply_reduce_fusion.3
  67.5 5.3 collective-permute-start.14
  72.8 1.9 collective-permute-start.13
  74.7 6.2 %collective-permute-start.12 = (f32[392,16]{0,1:T(8,128)S(1)}, f32[392,16]{0,1:T(8,128)S(1)}, u32[]{:S(2)}, u32[]{:S(2)}) collective-permute-start(f32[392,16]{0,1:T(8,128)S(1)} %get-tuple-element.28), channel_id=1, source_target_pairs={{0,16},{16,32},{32,48},{48,64},{64,80},{80,96},{96,112},{1,17},{17... | collective-permute-start | bytes 75272 | tf_op jit(solution)/shard_map/ppermute | solution.py:13
  89.1 2.4 collective-permute-start.8
  92.0 2.1 collective-permute-start.9
  95.5 5.6 %collective-permute-start.10 = (f32[384,256]{1,0:T(8,128)S(1)}, f32[384,256]{1,0:T(8,128)S(1)}, u32[]{:S(2)}, u32[]{:S(2)}) collective-permute-start(f32[384,256]{1,0:T(8,128)S(1)} %get-tuple-element.13), channel_id=1, source_target_pairs={{0,1},{1,2},{2,3},{3,4},{4,5},{5,6},{6,7},{7,8},{8,9},{9,10},{10,1... | collective-permute-start | bytes 1179656 | tf_op jit(solution)/shard_map/ppermute | solution.py:13
  105.0 6.7 %collective-permute-done.10 = f32[384,256]{1,0:T(8,128)S(1)} collective-permute-done((f32[384,256]{1,0:T(8,128)S(1)}, f32[384,256]{1,0:T(8,128)S(1)}, u32[]{:S(2)}, u32[]{:S(2)}) %collective-permute-start.10) | collective-permute-done | bytes 393248 | tf_op jit(solution)/shard_map/ppermute | solution.py:13
  113.0 8.0 %collective-permute-done.11 = f32[384,256]{1,0:T(8,128)S(1)} collective-permute-done((f32[384,256]{1,0:T(8,128)S(1)}, f32[384,256]{1,0:T(8,128)S(1)}, u32[]{:S(2)}, u32[]{:S(2)}) %collective-permute-start.11) | collective-permute-done | bytes 393248 | tf_op jit(solution)/shard_map/ppermute | solution.py:13
  122.2 1.6 reshape.277
  123.8 143.3 %all-gather.7.cloned.1.call-done = f32[66560,256]{1,0:T(8,128)} async-done(((f32[520,256]{1,0:T(8,128)}), f32[66560,256]{1,0:T(8,128)}) %all-gather.7.cloned.1.call-update) | async-done | bytes 68157456 | tf_op jit(solution)/shard_map/all_gather | solution.py:78
  267.1 22.0 %reduce_sum.87 = f32[520,256]{1,0:T(8,128)} reduce(f32[128,520,256]{2,1,0:T(8,128)} %bitcast.26, f32[]{:T(128)} %constant.10.clone.1), dimensions={0}, to_apply=%region_2.0 | reduce | flops 16906240 | bytes 68689920 | tf_op jit(solution)/shard_map/reduce_sum | solution.py:77
  289.1 1.9 slice.218
  291.0 2.0 copy.34
  293.0 3.2 fusion.35
  297.1 4.9 fusion.9
  302.0 7.4 %multiply_reduce_fusion.2 = (f32[256]{0:T(256)S(1)}, f32[1536,256]{1,0:T(8,128)S(1)}) fusion(f32[1536,256]{1,0:T(8,128)S(1)} %fusion.9, f32[1536]{0:T(1024)S(1)} %mul.194, f32[1,1,1536,1536]{3,2,1,0:T(8,128)} %param.9), kind=kOutput, calls=%fused_computation.34 | convolution fusion | flops 3625451264 | bytes 12590080 | tf_op jit(solution)/shard_map/dot_general | solution.py:88
  309.6 3.4 collective-permute-start.16
  313.0 1.9 collective-permute-start.17
  314.9 1.5 collective-permute-start.18
  316.4 1.5 collective-permute-start.19
  318.5 3.9 collective-permute-done.17
  324.9 3.6 collective-permute-done.19
  329.1 5.8 %multiply_reduce_fusion.1 = (f32[256]{0:T(256)S(1)}, f32[256]{0:T(256)S(1)}, f32[1536,256]{1,0:T(8,128)}) fusion(f32[1536]{0:T(1024)S(1)} %broadcast_multiply_fusion, f32[384,256]{1,0:T(8,128)S(1)} %convolution_subtract_fusion.8, f32[384,256]{1,0:T(8,128)S(1)} %convolution_subtract_fusion.9, f32[384,256]{1,0:T(8,128)S(1)} %convolution_subtract_fusion.10, ...), kind=kOutput, calls=%fused_computation.33 | convolution fusion | flops 3628596736 | bytes 14163968 | tf_op jit(solution)/shard_map/dot_general | solution.py:95
  336.8 4.4 collective-permute-start.20
  341.2 1.9 collective-permute-start.21
  343.1 3.2 collective-permute-start.22
  346.3 1.5 collective-permute-start.23
  354.4 5.3 collective-permute-done.23
  361.0 151.0 %all-gather.9.cloned.1.call-done = f32[66560,256]{1,0:T(8,128)} async-done(((f32[520,256]{1,0:T(8,128)}), f32[66560,256]{1,0:T(8,128)}) %all-gather.9.cloned.1.call-update) | async-done | bytes 68157456 | tf_op jit(solution)/shard_map/all_gather | solution.py:78
  512.0 21.1 %reduce_sum.93 = f32[520,256]{1,0:T(8,128)S(1)} reduce(f32[128,520,256]{2,1,0:T(8,128)} %bitcast.45, f32[]{:T(128)} %constant.10.clone.1), dimensions={0}, to_apply=%region_7.0 | reduce | flops 16906240 | bytes 68689920 | tf_op jit(solution)/shard_map/reduce_sum | solution.py:77
  536.2 6.7 %fusion.29 = f32[1,1,1536,256]{3,2,1,0:T(8,128)} fusion(f32[1536,256]{1,0:T(8,128)S(1)} %copy-done.28, f32[384,256]{1,0:T(8,128)} %convolution_subtract_fusion.4, f32[384,256]{1,0:T(8,128)} %convolution_subtract_fusion.5, f32[384,256]{1,0:T(8,128)} %convolution_subtract_fusion.6, f32[384,256]{1,0:T(8,128)} %convolution_subtract_fusion.7, ...), kind=kOutput, calls=%fused_computation.31 | convolution fusion | flops 2422603776 | bytes 9963520 | tf_op jit(solution)/shard_map/dot_general | solution.py:84
  (171 shorter events, 42.8 us)
Async XLA Ops:
  7.2 16.3 %copy-start.9 = (f32[1,1,1536,256]{3,2,1,0:T(8,128)S(1)}, f32[1,1,1536,256]{3,2,1,0:T(8,128)}, u32[]{:S(2)}) copy-start(f32[1,1,1536,256]{3,2,1,0:T(8,128)} %param.7) | copy-start | bytes 4718596
  7.2 15.6 %copy-start.32 = (s32[1,1,4,384]{3,2,1,0:T(4,128)S(1)}, s32[1,1,4,384]{3,2,1,0:T(4,128)}, u32[]{:S(2)}) copy-start(s32[1,1,4,384]{3,2,1,0:T(4,128)} %param.12) | copy-start | bytes 18436
  7.2 16.2 %copy-start.33 = (s32[1,1,16]{2,1,0:T(1,128)S(1)}, s32[1,1,16]{2,1,0:T(1,128)}, u32[]{:S(2)}) copy-start(s32[1,1,16]{2,1,0:T(1,128)} %param.11) | copy-start | bytes 196
  7.2 115.1 %all-gather.11.cloned.1.call-start = ((), (), s32[]{:S(2)}) async-start(), calls=%async_computation.2 | async-start | bytes 1056768 | tf_op jit(solution)/shard_map/all_gather | solution.py:54
  9.5 14.0 %collective-permute-start.3 = (f32[384,256]{1,0:T(8,128)}, f32[384,256]{1,0:T(8,128)}, u32[]{:S(2)}, u32[]{:S(2)}) collective-permute-start(f32[384,256]{1,0:T(8,128)} %get-tuple-element.23), channel_id=1, source_target_pairs={{1,0},{2,1},{3,2},{4,3},{5,4},{6,5},{7,6},{8,7},{9,8},{10,9},{11,1... | collective-permute-start | bytes 1179656 | tf_op jit(solution)/shard_map/ppermute | solution.py:13
  10.8 14.3 %collective-permute-start.2 = (f32[384,256]{1,0:T(8,128)S(1)}, f32[384,256]{1,0:T(8,128)}, u32[]{:S(2)}, u32[]{:S(2)}) collective-permute-start(f32[384,256]{1,0:T(8,128)S(1)} %get-tuple-element.22), channel_id=1, source_target_pairs={{0,1},{1,2},{2,3},{3,4},{4,5},{5,6},{6,7},{7,8},{8,9},{9,10},{10,1... | collective-permute-start | bytes 1179656 | tf_op jit(solution)/shard_map/ppermute | solution.py:13
  16.6 10.1 %collective-permute-start.1 = (f32[384,256]{1,0:T(8,128)S(1)}, f32[384,256]{1,0:T(8,128)}, u32[]{:S(2)}, u32[]{:S(2)}) collective-permute-start(f32[384,256]{1,0:T(8,128)S(1)} %get-tuple-element.21), channel_id=1, source_target_pairs={{16,0},{32,16},{48,32},{64,48},{80,64},{96,80},{112,96},{17,1},{33... | collective-permute-start | bytes 1179656 | tf_op jit(solution)/shard_map/ppermute | solution.py:13
  19.5 8.9 %collective-permute-start = (f32[384,256]{1,0:T(8,128)S(1)}, f32[384,256]{1,0:T(8,128)}, u32[]{:S(2)}, u32[]{:S(2)}) collective-permute-start(f32[384,256]{1,0:T(8,128)S(1)} %get-tuple-element.20), channel_id=1, source_target_pairs={{0,16},{16,32},{32,48},{48,64},{64,80},{80,96},{96,112},{1,17},{17... | collective-permute-start | bytes 1179656 | tf_op jit(solution)/shard_map/ppermute | solution.py:13
  22.7 244.4 %all-gather.7.cloned.1.call-start = ((), (), s32[]{:S(2)}) async-start(), calls=%async_computation | async-start | bytes 68689920 | tf_op jit(solution)/shard_map/all_gather | solution.py:78
  26.7 11.4 %copy-start.21 = (f32[384,256]{1,0:T(8,128)}, f32[384,256]{1,0:T(8,128)S(1)}, u32[]{:S(2)}) copy-start(f32[384,256]{1,0:T(8,128)S(1)} %convolution_subtract_fusion.21) | copy-start | bytes 1179652
  28.4 9.7 %copy-start.23 = (f32[384,256]{1,0:T(8,128)}, f32[384,256]{1,0:T(8,128)S(1)}, u32[]{:S(2)}) copy-start(f32[384,256]{1,0:T(8,128)S(1)} %convolution_subtract_fusion.22) | copy-start | bytes 1179652
  30.1 8.1 %copy-start.25 = (f32[384,256]{1,0:T(8,128)}, f32[384,256]{1,0:T(8,128)S(1)}, u32[]{:S(2)}) copy-start(f32[384,256]{1,0:T(8,128)S(1)} %convolution_subtract_fusion.23) | copy-start | bytes 1179652
  30.1 30.5 %slice-start = ((s8[9437184]{0:T(1024)(128)(4,1)}), s8[4194304]{0:T(1024)(128)(4,1)S(1)}, s32[]{:S(2)}) async-start(s8[9437184]{0:T(1024)(128)(4,1)} %bitcast.174), calls=%async_computation.3 | async-start | bytes 8388608
  30.1 30.5 %slice-start.1 = ((s8[9437184]{0:T(1024)(128)(4,1)}), s8[4194304]{0:T(1024)(128)(4,1)S(1)}, s32[]{:S(2)}) async-start(s8[9437184]{0:T(1024)(128)(4,1)} %bitcast.174), calls=%async_computation.4 | async-start | bytes 8388608
  38.1 22.5 %slice-start.2 = ((s8[9437184]{0:T(1024)(128)(4,1)}), s8[1048576]{0:T(1024)(128)(4,1)S(1)}, s32[]{:S(2)}) async-start(s8[9437184]{0:T(1024)(128)(4,1)} %bitcast.174), calls=%async_computation.5 | async-start | bytes 2097152
  38.3 11.4 %collective-permute-start.4 = (f32[384,256]{1,0:T(8,128)S(1)}, f32[384,256]{1,0:T(8,128)S(1)}, u32[]{:S(2)}, u32[]{:S(2)}) collective-permute-start(f32[384,256]{1,0:T(8,128)S(1)} %get-tuple-element.16), channel_id=1, source_target_pairs={{0,16},{16,32},{32,48},{48,64},{64,80},{80,96},{96,112},{1,17},{17... | collective-permute-start | bytes 1179656 | tf_op jit(solution)/shard_map/ppermute | solution.py:13
  42.3 9.4 %collective-permute-start.5 = (f32[384,256]{1,0:T(8,128)S(1)}, f32[384,256]{1,0:T(8,128)S(1)}, u32[]{:S(2)}, u32[]{:S(2)}) collective-permute-start(f32[384,256]{1,0:T(8,128)S(1)} %get-tuple-element.19), channel_id=1, source_target_pairs={{16,0},{32,16},{48,32},{64,48},{80,64},{96,80},{112,96},{17,1},{33... | collective-permute-start | bytes 1179656 | tf_op jit(solution)/shard_map/ppermute | solution.py:13
  44.2 10.5 %collective-permute-start.6 = (f32[384,256]{1,0:T(8,128)S(1)}, f32[384,256]{1,0:T(8,128)S(1)}, u32[]{:S(2)}, u32[]{:S(2)}) collective-permute-start(f32[384,256]{1,0:T(8,128)S(1)} %get-tuple-element.17), channel_id=1, source_target_pairs={{0,1},{1,2},{2,3},{3,4},{4,5},{5,6},{6,7},{7,8},{8,9},{9,10},{10,1... | collective-permute-start | bytes 1179656 | tf_op jit(solution)/shard_map/ppermute | solution.py:13
  47.8 11.6 %collective-permute-start.7 = (f32[384,256]{1,0:T(8,128)S(1)}, f32[384,256]{1,0:T(8,128)S(1)}, u32[]{:S(2)}, u32[]{:S(2)}) collective-permute-start(f32[384,256]{1,0:T(8,128)S(1)} %get-tuple-element.18), channel_id=1, source_target_pairs={{1,0},{2,1},{3,2},{4,3},{5,4},{6,5},{7,6},{8,7},{9,8},{10,9},{11,1... | collective-permute-start | bytes 1179656 | tf_op jit(solution)/shard_map/ppermute | solution.py:13
  50.2 10.4 %copy-start.1 = (f32[384,256]{1,0:T(8,128)}, f32[384,256]{1,0:T(8,128)S(1)}, u32[]{:S(2)}) copy-start(f32[384,256]{1,0:T(8,128)S(1)} %convolution_subtract_fusion.19) | copy-start | bytes 1179652
  52.2 8.3 %copy-start.3 = (f32[384,256]{1,0:T(8,128)}, f32[384,256]{1,0:T(8,128)S(1)}, u32[]{:S(2)}) copy-start(f32[384,256]{1,0:T(8,128)S(1)} %convolution_subtract_fusion.18) | copy-start | bytes 1179652
  52.2 7.7 %copy-start.31 = (f32[1,1,16,1536]{3,2,1,0:T(8,128)S(1)}, f32[1,1,16,1536]{3,2,1,0:T(8,128)}, u32[]{:S(2)}) copy-start(f32[1,1,16,1536]{3,2,1,0:T(8,128)} %param.10) | copy-start | bytes 294916
  66.0 446.0 %all-gather.9.cloned.1.call-start = ((), (), s32[]{:S(2)}) async-start(), calls=%async_computation.1 | async-start | bytes 68689920 | tf_op jit(solution)/shard_map/all_gather | solution.py:78
  66.2 16.8 %collective-permute-start.15 = (f32[392,16]{0,1:T(8,128)S(1)}, f32[392,16]{0,1:T(8,128)S(1)}, u32[]{:S(2)}, u32[]{:S(2)}) collective-permute-start(f32[392,16]{0,1:T(8,128)S(1)} %get-tuple-element.31), channel_id=1, source_target_pairs={{1,0},{2,1},{3,2},{4,3},{5,4},{6,5},{7,6},{8,7},{9,8},{10,9},{11,1... | collective-permute-start | bytes 75272 | tf_op jit(solution)/shard_map/ppermute | solution.py:13
  67.5 15.7 %collective-permute-start.14 = (f32[392,16]{0,1:T(8,128)S(1)}, f32[392,16]{0,1:T(8,128)S(1)}, u32[]{:S(2)}, u32[]{:S(2)}) collective-permute-start(f32[392,16]{0,1:T(8,128)S(1)} %get-tuple-element.30), channel_id=1, source_target_pairs={{0,1},{1,2},{2,3},{3,4},{4,5},{5,6},{6,7},{7,8},{8,9},{9,10},{10,1... | collective-permute-start | bytes 75272 | tf_op jit(solution)/shard_map/ppermute | solution.py:13
  72.8 10.5 %collective-permute-start.13 = (f32[392,16]{0,1:T(8,128)S(1)}, f32[392,16]{0,1:T(8,128)S(1)}, u32[]{:S(2)}, u32[]{:S(2)}) collective-permute-start(f32[392,16]{0,1:T(8,128)S(1)} %get-tuple-element.29), channel_id=1, source_target_pairs={{16,0},{32,16},{48,32},{64,48},{80,64},{96,80},{112,96},{17,1},{33... | collective-permute-start | bytes 75272 | tf_op jit(solution)/shard_map/ppermute | solution.py:13
  74.7 16.7 %collective-permute-start.12 = (f32[392,16]{0,1:T(8,128)S(1)}, f32[392,16]{0,1:T(8,128)S(1)}, u32[]{:S(2)}, u32[]{:S(2)}) collective-permute-start(f32[392,16]{0,1:T(8,128)S(1)} %get-tuple-element.28), channel_id=1, source_target_pairs={{0,16},{16,32},{32,48},{48,64},{64,80},{80,96},{96,112},{1,17},{17... | collective-permute-start | bytes 75272 | tf_op jit(solution)/shard_map/ppermute | solution.py:13
  89.1 13.3 %collective-permute-start.8 = (f32[384,256]{1,0:T(8,128)S(1)}, f32[384,256]{1,0:T(8,128)S(1)}, u32[]{:S(2)}, u32[]{:S(2)}) collective-permute-start(f32[384,256]{1,0:T(8,128)S(1)} %get-tuple-element.12), channel_id=1, source_target_pairs={{0,16},{16,32},{32,48},{48,64},{64,80},{80,96},{96,112},{1,17},{17... | collective-permute-start | bytes 1179656 | tf_op jit(solution)/shard_map/ppermute | solution.py:13
  92.0 11.7 %collective-permute-start.9 = (f32[384,256]{1,0:T(8,128)S(1)}, f32[384,256]{1,0:T(8,128)S(1)}, u32[]{:S(2)}, u32[]{:S(2)}) collective-permute-start(f32[384,256]{1,0:T(8,128)S(1)} %get-tuple-element.15), channel_id=1, source_target_pairs={{16,0},{32,16},{48,32},{64,48},{80,64},{96,80},{112,96},{17,1},{33... | collective-permute-start | bytes 1179656 | tf_op jit(solution)/shard_map/ppermute | solution.py:13
  95.5 16.2 %collective-permute-start.10 = (f32[384,256]{1,0:T(8,128)S(1)}, f32[384,256]{1,0:T(8,128)S(1)}, u32[]{:S(2)}, u32[]{:S(2)}) collective-permute-start(f32[384,256]{1,0:T(8,128)S(1)} %get-tuple-element.13), channel_id=1, source_target_pairs={{0,1},{1,2},{2,3},{3,4},{4,5},{5,6},{6,7},{7,8},{8,9},{9,10},{10,1... | collective-permute-start | bytes 1179656 | tf_op jit(solution)/shard_map/ppermute | solution.py:13
  101.1 19.9 %collective-permute-start.11 = (f32[384,256]{1,0:T(8,128)S(1)}, f32[384,256]{1,0:T(8,128)S(1)}, u32[]{:S(2)}, u32[]{:S(2)}) collective-permute-start(f32[384,256]{1,0:T(8,128)S(1)} %get-tuple-element.14), channel_id=1, source_target_pairs={{1,0},{2,1},{3,2},{4,3},{5,4},{6,5},{7,6},{8,7},{9,8},{10,9},{11,1... | collective-permute-start | bytes 1179656 | tf_op jit(solution)/shard_map/ppermute | solution.py:13
  302.0 7.5 %copy-start.27 = (f32[1536,256]{1,0:T(8,128)}, f32[1536,256]{1,0:T(8,128)S(1)}, u32[]{:S(2)}) copy-start(f32[1536,256]{1,0:T(8,128)S(1)} %fusion.9) | copy-start | bytes 4718596
  302.0 27.0 %slice-start.3 = ((s8[9437184]{0:T(1024)(128)(4,1)}), s8[4194304]{0:T(1024)(128)(4,1)S(1)}, s32[]{:S(2)}) async-start(s8[9437184]{0:T(1024)(128)(4,1)} %bitcast.176), calls=%async_computation.6 | async-start | bytes 8388608
  302.0 27.0 %slice-start.4 = ((s8[9437184]{0:T(1024)(128)(4,1)}), s8[4194304]{0:T(1024)(128)(4,1)S(1)}, s32[]{:S(2)}) async-start(s8[9437184]{0:T(1024)(128)(4,1)} %bitcast.176), calls=%async_computation.7 | async-start | bytes 8388608
  309.5 19.5 %slice-start.5 = ((s8[9437184]{0:T(1024)(128)(4,1)}), s8[1048576]{0:T(1024)(128)(4,1)S(1)}, s32[]{:S(2)}) async-start(s8[9437184]{0:T(1024)(128)(4,1)} %bitcast.176), calls=%async_computation.8 | async-start | bytes 2097152
  309.6 8.3 %collective-permute-start.16 = (f32[384,256]{1,0:T(8,128)S(1)}, f32[384,256]{1,0:T(8,128)S(1)}, u32[]{:S(2)}, u32[]{:S(2)}) collective-permute-start(f32[384,256]{1,0:T(8,128)S(1)} %get-tuple-element.8), channel_id=1, source_target_pairs={{0,16},{16,32},{32,48},{48,64},{64,80},{80,96},{96,112},{1,17},{17... | collective-permute-start | bytes 1179656 | tf_op jit(solution)/shard_map/ppermute | solution.py:13
  313.0 9.4 %collective-permute-start.17 = (f32[384,256]{1,0:T(8,128)S(1)}, f32[384,256]{1,0:T(8,128)S(1)}, u32[]{:S(2)}, u32[]{:S(2)}) collective-permute-start(f32[384,256]{1,0:T(8,128)S(1)} %get-tuple-element.11), channel_id=1, source_target_pairs={{16,0},{32,16},{48,32},{64,48},{80,64},{96,80},{112,96},{17,1},{33... | collective-permute-start | bytes 1179656 | tf_op jit(solution)/shard_map/ppermute | solution.py:13
  314.9 9.4 %collective-permute-start.18 = (f32[384,256]{1,0:T(8,128)S(1)}, f32[384,256]{1,0:T(8,128)S(1)}, u32[]{:S(2)}, u32[]{:S(2)}) collective-permute-start(f32[384,256]{1,0:T(8,128)S(1)} %get-tuple-element.9), channel_id=1, source_target_pairs={{0,1},{1,2},{2,3},{3,4},{4,5},{5,6},{6,7},{7,8},{8,9},{9,10},{10,1... | collective-permute-start | bytes 1179656 | tf_op jit(solution)/shard_map/ppermute | solution.py:13
  316.4 12.0 %collective-permute-start.19 = (f32[384,256]{1,0:T(8,128)S(1)}, f32[384,256]{1,0:T(8,128)S(1)}, u32[]{:S(2)}, u32[]{:S(2)}) collective-permute-start(f32[384,256]{1,0:T(8,128)S(1)} %get-tuple-element.10), channel_id=1, source_target_pairs={{1,0},{2,1},{3,2},{4,3},{5,4},{6,5},{7,6},{8,7},{9,8},{10,9},{11,1... | collective-permute-start | bytes 1179656 | tf_op jit(solution)/shard_map/ppermute | solution.py:13
  318.5 16.3 %copy-start.10 = (f32[384,256]{1,0:T(8,128)}, f32[384,256]{1,0:T(8,128)S(1)}, u32[]{:S(2)}) copy-start(f32[384,256]{1,0:T(8,128)S(1)} %convolution_subtract_fusion.11) | copy-start | bytes 1179652
  322.9 11.9 %copy-start.12 = (f32[384,256]{1,0:T(8,128)}, f32[384,256]{1,0:T(8,128)S(1)}, u32[]{:S(2)}) copy-start(f32[384,256]{1,0:T(8,128)S(1)} %convolution_subtract_fusion.10) | copy-start | bytes 1179652
  324.9 10.0 %copy-start.14 = (f32[384,256]{1,0:T(8,128)}, f32[384,256]{1,0:T(8,128)S(1)}, u32[]{:S(2)}) copy-start(f32[384,256]{1,0:T(8,128)S(1)} %convolution_subtract_fusion.9) | copy-start | bytes 1179652
  336.8 11.1 %collective-permute-start.20 = (f32[384,256]{1,0:T(8,128)S(1)}, f32[384,256]{1,0:T(8,128)S(1)}, u32[]{:S(2)}, u32[]{:S(2)}) collective-permute-start(f32[384,256]{1,0:T(8,128)S(1)} %get-tuple-element.4), channel_id=1, source_target_pairs={{0,16},{16,32},{32,48},{48,64},{64,80},{80,96},{96,112},{1,17},{17... | collective-permute-start | bytes 1179656 | tf_op jit(solution)/shard_map/ppermute | solution.py:13
  341.2 9.4 %collective-permute-start.21 = (f32[384,256]{1,0:T(8,128)S(1)}, f32[384,256]{1,0:T(8,128)S(1)}, u32[]{:S(2)}, u32[]{:S(2)}) collective-permute-start(f32[384,256]{1,0:T(8,128)S(1)} %get-tuple-element.7), channel_id=1, source_target_pairs={{16,0},{32,16},{48,32},{64,48},{80,64},{96,80},{112,96},{17,1},{33... | collective-permute-start | bytes 1179656 | tf_op jit(solution)/shard_map/ppermute | solution.py:13
  343.1 10.0 %collective-permute-start.22 = (f32[384,256]{1,0:T(8,128)S(1)}, f32[384,256]{1,0:T(8,128)S(1)}, u32[]{:S(2)}, u32[]{:S(2)}) collective-permute-start(f32[384,256]{1,0:T(8,128)S(1)} %get-tuple-element.5), channel_id=1, source_target_pairs={{0,1},{1,2},{2,3},{3,4},{4,5},{5,6},{6,7},{7,8},{8,9},{9,10},{10,1... | collective-permute-start | bytes 1179656 | tf_op jit(solution)/shard_map/ppermute | solution.py:13
  346.3 13.3 %collective-permute-start.23 = (f32[384,256]{1,0:T(8,128)S(1)}, f32[384,256]{1,0:T(8,128)S(1)}, u32[]{:S(2)}, u32[]{:S(2)}) collective-permute-start(f32[384,256]{1,0:T(8,128)S(1)} %get-tuple-element.6), channel_id=1, source_target_pairs={{1,0},{2,1},{3,2},{4,3},{5,4},{6,5},{7,6},{8,7},{9,8},{10,9},{11,1... | collective-permute-start | bytes 1179656 | tf_op jit(solution)/shard_map/ppermute | solution.py:13
  536.1 6.7 %copy-start.2 = (f32[384,256]{1,0:T(8,128)S(1)}, f32[384,256]{1,0:T(8,128)}, u32[]{:S(2)}) copy-start(f32[384,256]{1,0:T(8,128)} %copy-done.1) | copy-start | bytes 1179652
  536.1 6.7 %copy-start.4 = (f32[384,256]{1,0:T(8,128)S(1)}, f32[384,256]{1,0:T(8,128)}, u32[]{:S(2)}) copy-start(f32[384,256]{1,0:T(8,128)} %copy-done.3) | copy-start | bytes 1179652
  (19 other events, 88.5 us)
Sparse Core Ops, SparseCore 0:
  22.8 72.3 all-gather.10
  98.7 168.3 all-gather.6
  336.8 175.1 all-gather.8
